TPU v7x, 1024 devices: a whole 4x4x32 slice. The times are simulated.
1024 devices in a mesh: sub: 256 (over y, z, core), grp: 4 (over x).
Axes of the slice: x: 4, y: 4, z: 32, core: 2. Of those that a mesh axis runs over, the one named last changes fastest.
Arguments:
- dual_ops: float32 [256, 4, 576, 576], P('sub', 'grp'), as said below
- gap_parts: float32 [256, 4, 576, 256], P('sub', 'grp')
- modes: float32 [256, 4, 576, 48], P('sub', 'grp'), may hold values from -0.25 to 0.25
- coarse_rows: float32 [256, 4, 48, 192], P('sub', 'grp'), as said below
- face_live: int32 [256, 4, 6], P('sub', 'grp'), may hold values from 0 to 1, as said below
- contact: int32 [256, 4, 6], P('sub', 'grp'), may hold values from 0 to 1, as said below
Outputs:
- multipliers: float32 [256, 4, 576, 256], P('sub', 'grp')
- direction: float32 [256, 4, 576, 256], P('sub', 'grp')
Inputs may be any that keep to these rules, and one draw needn't show every extreme that they name: Slot k of face_live is 1 only where the subdomain across slot k exists in the geometry (slots 0 and 1 stay within one row of 16 subdomains along sub), and it equals the flag of slot k XOR 1 of that subdomain; face blocks across a shared face list the same points in the same order. `contact`: 1 only where face_live is 1, and equal on both sides of a face. `dual_ops`: each subdomain's block is symmetric positive definite. `coarse_rows`: for each index along sub, the rows of the 4 subdomains stacked in grp order form a symmetric matrix.
All inputs are finite; a program needn't handle non-finite values.
Results may differ from a plain program's by a relative error of at most 0.00012.
Values sent between devices are 32-bit elements; how exact they have to be, the bound alone decides.
No kernel may reach another device: no remote copies, remote signals or barrier semaphores. Data moves between devices by JAX's collectives and lax.ppermute only.
A program may use at most 32 MiB of HBM per device.

v0:
```python
import functools
import math

import jax
import jax.numpy as jnp
from jax import lax
from jax.experimental import pallas as pl
from jax.experimental.pallas import tpu as pltpu
from jax.sharding import Mesh, PartitionSpec as P


SUBROW = 16
SLOTS = 6
LANES = 128
CORE = 6
PLANE = ("y", "core", "grp")
SUB = ("y", "z", "core")
SOURCES = ((SUB, -1), (SUB, 1), (SUB, -SUBROW), (SUB, SUBROW), ("grp", -1), ("grp", 1))
ORDER = (2, 3, 1, 4, 5, 0)


def fetch(piece, slot):
    axis, offset = SOURCES[slot]
    count = lax.axis_size(axis)
    turned = [1 - 2 * (i % 2) if axis == SUB else 1 for i in range(count)]
    pairs = [(i, i - offset * turned[i]) for i in range(count) if 0 <= i - offset * turned[i] < count]
    return lax.ppermute(piece, axis, pairs)


def exchange(pieces):
    gotten = [None] * len(pieces)
    for slot in ORDER:
        if slot < len(pieces):
            gotten[slot] = fetch(pieces[slot], slot)
    return gotten


def swap(blocks, axes):
    return lax.all_to_all(blocks, axes, 0, 0, tiled=True)


def total(terms):
    plane = lax.axis_size(PLANE)
    chunks = terms.reshape(plane, -1)
    chunk = jnp.sum(swap(chunks, PLANE), axis=0)
    chunk = jnp.sum(swap(jnp.broadcast_to(chunk, (lax.axis_size("z"),) + chunk.shape), "z"), axis=0)
    return swap(jnp.broadcast_to(chunk, chunks.shape), PLANE)[:, None]


def dot(left, right, across=1):
    return lax.dot_general(
        left, right, (((across,), (0,)), ((), ())),
        precision=lax.Precision.HIGHEST, preferred_element_type=jnp.float32,
    )


def clamp(values, slot, touching):
    bounded = jnp.maximum(values, 0.0) if slot % 2 else jnp.minimum(values, 0.0)
    return jnp.where(touching, bounded, values)


def kernel_call(body, flags, arrays, outs, flops):
    smem = pl.BlockSpec(memory_space=pltpu.SMEM)
    vmem = pl.BlockSpec(memory_space=pltpu.VMEM)
    moved = sum(a.size for a in arrays) + sum(math.prod(o) for o in outs)
    return pl.pallas_call(
        functools.partial(body, len(flags), len(arrays)),
        out_shape=[jax.ShapeDtypeStruct(o, jnp.float32) for o in outs],
        in_specs=[smem] * len(flags) + [vmem] * len(arrays),
        out_specs=[vmem] * len(outs),
        compiler_params=pltpu.CompilerParams(vmem_limit_bytes=24 << 20),
        cost_estimate=pl.CostEstimate(flops=flops, bytes_accessed=4 * moved, transcendentals=0),
    )(*flags, *arrays)


def split(refs, flags, arrays):
    return refs[:flags], refs[flags:flags + arrays], refs[flags + arrays:]


def unturned(second, arrays, received):
    turned = []
    for lower, upper in ((0, 1), (2, 3)):
        low, up = arrays[lower], arrays[upper]
        if received and lower == 0:
            low, up = up, low
        turned.append(jnp.where(second, up, low))
        turned.append(jnp.where(second, low, up))
    return turned + list(arrays[4:])


def pack_kernel(gap, shapes, rows, *refs):
    outs, (shapes_here, rows_here, sems) = refs[:SLOTS], refs[SLOTS:]
    face = gap.shape[0] // SLOTS
    half = shapes.shape[0] // 2
    core = lax.axis_index("core")
    copies = [
        pltpu.make_async_copy(shapes, shapes_here, sems.at[0]),
        pltpu.make_async_copy(rows, rows_here, sems.at[1]),
    ]
    for slot, out in enumerate(outs):
        turn = 0 if slot >= 4 else core if slot % 2 else -core
        at = ((slot ^ 1) + turn) * face
        piece = gap.at[pl.ds(pl.multiple_of(at, 8), face)]
        copies.append(pltpu.make_async_copy(piece, out.at[pl.ds(0, face)], sems.at[2 + slot]))
    for copy in copies:
        copy.start()
    copies[0].wait()
    second = jnp.full((shapes.shape[0], face), core, jnp.int32) > 0
    pieces = [shapes_here[:, slot * face:(slot + 1) * face] for slot in range(SLOTS)]
    pieces = unturned(second, [pieces[slot ^ 1] for slot in range(SLOTS)], False)
    for piece, out in zip(pieces, outs):
        out[face:face + half] = jnp.zeros((half, out.shape[1]), jnp.float32)
        out[face:face + half, :face] = piece[:half]
        out[face:face + half, LANES:LANES + face] = piece[half:]
    copies[1].wait()
    for out in outs[4:]:
        out[face + half:] = jnp.zeros((2 * half, out.shape[1]), jnp.float32)
        out[face + half:, :rows.shape[1]] = rows_here[...]
    for copy in copies[2:]:
        copy.wait()


def pack(gap, shapes, rows):
    face = gap.shape[0] // SLOTS
    short = face + shapes.shape[0] // 2
    heights = [short] * 4 + [short + shapes.shape[0]] * 2
    hbm = pl.BlockSpec(memory_space=pltpu.HBM)
    vmem = pl.BlockSpec(memory_space=pltpu.VMEM)
    return pl.pallas_call(
        pack_kernel,
        out_shape=[jax.ShapeDtypeStruct((height, gap.shape[1]), jnp.float32) for height in heights],
        in_specs=[hbm] * 3,
        out_specs=[vmem] * SLOTS,
        scratch_shapes=[
            pltpu.VMEM(shapes.shape, jnp.float32), pltpu.VMEM(rows.shape, jnp.float32),
            pltpu.SemaphoreType.DMA((2 + SLOTS,)),
        ],
        compiler_params=pltpu.CompilerParams(vmem_limit_bytes=67043328),
        name="pack",
    )(gap, shapes, rows)


def flags_kernel(nf, na, *refs):
    (live, contact), (gap, shapes), (flags, masked, kept) = split(refs, nf, na)
    face = gap.shape[0] // SLOTS
    flags[CORE:CORE + 1] = jnp.full((1, flags.shape[1]), lax.axis_index("core"), jnp.int32).astype(jnp.float32)
    for slot in range(SLOTS):
        shape = (1, flags.shape[1])
        rows = slice(slot * face, (slot + 1) * face)
        flags[slot:slot + 1] = jnp.full(shape, live[0, slot], jnp.int32).astype(jnp.float32)
        flags[8 + slot:9 + slot] = jnp.full(shape, contact[0, slot], jnp.int32).astype(jnp.float32)
        masked[rows] = flags[slot:slot + 1] * gap[rows]
    kept[...] = shapes[...]


def residual_kernel(nf, na, *refs):
    _, (flags, masked, shapes, *messages), (values, spread) = split(refs, nf, na)
    face = values.shape[0] // SLOTS
    gotten = unturned(flags[CORE:CORE + 1] > 0.0, [message[:face] for message in messages], True)
    for slot in range(SLOTS):
        rows = slice(slot * face, (slot + 1) * face)
        values[rows] = flags[slot:slot + 1] * gotten[slot] - masked[rows]
    coef = dot(shapes[...], values[...])
    for row in range(spread.shape[0]):
        spread[row] = coef


def opened_kernel(nf, na, *refs):
    _, (flags, shapes, *faces), (values, spread) = split(refs, nf, na)
    second = flags[CORE:CORE + 1] > 0.0
    gotten = unturned(second, [array[...] for array in faces[SLOTS:]], True)
    sent = unturned(second, [array[...] for array in faces[:SLOTS]], False)
    face = values.shape[0] // SLOTS
    for slot in range(SLOTS):
        rows = slice(slot * face, (slot + 1) * face)
        values[rows] = flags[slot:slot + 1] * (sent[slot ^ 1] - gotten[slot])
    coef = dot(shapes[...], values[...])
    for row in range(spread.shape[0]):
        spread[row] = coef


def coarse_kernel(nf, na, *refs):
    _, (rows, coefs), (own,) = split(refs, nf, na)
    own[...] = dot(rows[...], coefs[...])


def pairs_kernel(nf, na, *refs):
    (live,), (flags, shapes, *messages), (pairs,) = split(refs, nf, na)
    face = pairs.shape[0] // SLOTS
    half = shapes.shape[0] // 2
    packs = unturned(flags[CORE:CORE + 1] > 0.0, [message[face:face + half] for message in messages], True)
    for slot in range(SLOTS):
        rows = slice(slot * face, (slot + 1) * face)
        packed = packs[slot]
        both = jnp.concatenate([shapes[:, rows], -packed[:, :face], -packed[:, LANES:LANES + face]])
        pairs[rows] = live[0, slot].astype(jnp.float32) * both.T


def beside_kernel(nf, na, *refs):
    _, (coefs, *messages), outs = split(refs, nf, na)
    for message, out in zip(messages, outs):
        out[...] = dot(message[message.shape[0] - out.shape[0]:, :coefs.shape[0]], coefs[...])


def corrected(flags, values, pairs, own, near):
    face = values.shape[0] // SLOTS
    near = unturned(flags[CORE:CORE + 1] > 0.0, [array[...] for array in near], True)
    faces = []
    for slot in range(SLOTS):
        rows = slice(slot * face, (slot + 1) * face)
        faces.append(values[rows] - dot(pairs[rows], jnp.concatenate([own[...], near[slot]])))
    return faces


def push_kernel(nf, na, *refs):
    _, (flags, values, operator, pairs, own, *near), (first, push, *far) = split(refs, nf, na)
    face = values.shape[0] // SLOTS
    for slot, part in enumerate(corrected(flags, values, pairs, own, near)):
        rows = slice(slot * face, (slot + 1) * face)
        first[rows] = part
        push[rows] = clamp(-part, slot, flags[8 + slot:9 + slot] > 0.0)
    image = dot(operator[2 * face:4 * face], push[...])
    second = flags[CORE:CORE + 1] > 0.0
    lower, upper = image[:face], image[face:]
    far[0][...] = jnp.where(second, lower, upper)
    far[1][...] = jnp.where(second, upper, lower)


def rest_kernel(nf, na, *refs):
    _, (flags, operator, push), outs = split(refs, nf, na)
    second = flags[CORE:CORE + 1] > 0.0
    face = operator.shape[0] // SLOTS
    upper = dot(operator[:2 * face], push[...])
    lower = dot(operator[4 * face:], push[...])
    outs[0][...] = jnp.where(second, upper[:face], upper[face:])
    outs[1][...] = jnp.where(second, upper[face:], upper[:face])
    outs[2][...] = lower[face:]
    outs[3][...] = lower[:face]


def inner(left, right):
    return jnp.sum(left * right, axis=0, keepdims=True)


def image_kernel(nf, na, *refs):
    _, (operator, first), (image, sums) = split(refs, nf, na)
    image[...] = dot(operator[...], first[...])
    sums[0:1] = inner(first[...], first[...])
    sums[1:2] = inner(first[...], image[...])


def change_kernel(nf, na, *refs):
    _, (flags, values, operator, pairs, first, image, early, own, *near), (change, sums) = split(refs, nf, na)
    face = values.shape[0] // SLOTS
    for slot, part in enumerate(corrected(flags, values, pairs, own, near)):
        change[slot * face:(slot + 1) * face] = part
    moved = dot(operator[...], change[...])
    sums[0:2] = early[...]
    sums[2:3] = inner(first[...], change[...])
    sums[3:4] = inner(change[...], change[...])
    sums[4:5] = inner(change[...], image[...])
    sums[5:6] = inner(change[...], moved)


def finish_kernel(nf, na, *refs):
    _, (flags, sums, first, push, change), (multipliers, direction) = split(refs, nf, na)
    face = first.shape[0] // SLOTS
    flat = jnp.concatenate([sums[i] for i in range(sums.shape[0])], axis=1)
    cases = first.shape[1]
    s = [flat[:, i * cases:(i + 1) * cases] for i in range(6)]
    step = s[0] / (2.0 * s[1])
    norm = s[0] + step * (2.0 * s[2] + step * s[3])
    curvature = 2.0 * (s[1] + step * (2.0 * s[4] + step * s[5]))
    ratio = norm / curvature
    for slot in range(SLOTS):
        rows = slice(slot * face, (slot + 1) * face)
        part = first[rows] + step * change[rows]
        direction[rows] = part
        multipliers[rows] = clamp(step * push[rows] - ratio * part, slot, flags[8 + slot:9 + slot] > 0.0)


def body(dual_ops, gap_parts, modes, coarse_rows, face_live, contact):
    operator = dual_ops[0, 0]
    dual_rows = operator.shape[0]
    face = dual_rows // SLOTS
    cases = gap_parts.shape[3]
    kinds = modes.shape[3]
    groups = lax.axis_size("grp")
    live, touching = face_live[0], contact[0]
    rows = coarse_rows[0, 0]
    parts = gap_parts[0, 0]
    shapes = modes[0, 0].T
    whole = (dual_rows, cases)
    spread = (groups, kinds, cases)
    heavy = 12 * dual_rows * dual_rows * cases
    light = 12 * dual_rows * kinds * cases

    messages = exchange(pack(parts, shapes, rows))
    flags, masked, shapes = kernel_call(
        flags_kernel, [live, touching], [parts, shapes], [(16, cases), whole, shapes.shape], 0
    )

    def coarse(spread_coef):
        coefs = swap(spread_coef, "grp").reshape(groups * kinds, cases)
        own, = kernel_call(coarse_kernel, [], [rows, coefs], [(kinds, cases)], light // 3)
        near = exchange([own] * 4)
        beside = kernel_call(beside_kernel, [], [coefs, *messages[4:]], [(kinds, cases)] * 2, light)
        return [own, *near, *beside]

    values, coef = kernel_call(residual_kernel, [], [flags, masked, shapes, *messages], [whole, spread], light)
    known = coarse(coef)
    pairs, = kernel_call(pairs_kernel, [live], [flags, shapes, *messages], [(dual_rows, 2 * kinds)], light)
    first, push, *far = kernel_call(
        push_kernel, [], [flags, values, operator, pairs, *known], [whole, whole] + [(face, cases)] * 2,
        heavy // 3 + 2 * light,
    )
    rest = kernel_call(rest_kernel, [], [flags, operator, push], [(face, cases)] * 4, 2 * heavy // 3)
    sent = [*rest[:2], *far, *rest[2:]]
    gotten = exchange(sent)
    image, early = kernel_call(image_kernel, [], [operator, first], [whole, (2, cases)], heavy)
    values, coef = kernel_call(opened_kernel, [], [flags, shapes, *sent, *gotten], [whole, spread], light)
    known = coarse(coef)
    change, sums = kernel_call(
        change_kernel, [], [flags, values, operator, pairs, first, image, early, *known],
        [whole, (6, cases)], heavy + 2 * light,
    )
    multipliers, direction = kernel_call(
        finish_kernel, [], [flags, total(sums), first, push, change], [whole, whole], 8 * dual_rows * cases
    )
    shape = (1, 1) + whole
    return (multipliers.reshape(shape), direction.reshape(shape))


def solution(mesh):
    fine = Mesh(mesh.devices.reshape(4, 32, 2, 4), ("y", "z", "core", "grp"))
    wide = P(SUB, "grp", None, None)
    flags = P(SUB, "grp", None)
    return jax.shard_map(
        body, mesh=fine, in_specs=(wide, wide, wide, wide, flags, flags), out_specs=(wide, wide), check_vma=False
    )
```

profile of v0, /device:TPU:1, one launch (start us, length us, event | category | flops | bytes accessed | tf_op | source)
XLA Modules:
  0.0 224.7 jit_solution(6206708331896804170)
XLA Ops:
  0.6 2.2 pack.1
  2.8 16.0 %collective-permute-start = (f32[120,256]{1,0:T(8,128)}, f32[120,256]{1,0:T(8,128)S(1)}, u32[]{:S(2)}, u32[]{:S(2)}) collective-permute-start(f32[120,256]{1,0:T(8,128)} %get-tuple-element.36), channel_id=1, source_target_pairs={{0,4},{4,0},{8,12},{12,8},{16,20},{20,16},{24,28},{28,24},{32,36},... | collective-permute-start | bytes 368648 | tf_op jit(solution)/shard_map/ppermute | solution.py:27
  18.8 1.3 collective-permute-start.4
  20.1 1.3 collective-permute-start.5
  21.4 1.9 collective-permute-start.1
  23.4 1.3 collective-permute-start.2
  24.7 0.0 collective-permute-done.refs_3_
  24.7 12.7 %collective-permute-start.3 = (f32[120,256]{1,0:T(8,128)}, f32[120,256]{1,0:T(8,128)S(1)}, u32[]{:S(2)}, u32[]{:S(2)}) collective-permute-start(f32[120,256]{1,0:T(8,128)} %get-tuple-element.39), channel_id=1, source_target_pairs={{4,68},{12,76},{20,84},{28,92},{36,100},{44,108},{52,116},{60,124}... | collective-permute-start | bytes 368648 | tf_op jit(solution)/shard_map/ppermute | solution.py:27
  37.4 0.0 copy-start
  37.4 1.1 copy-done
  38.5 0.9 copy-done.2
  39.4 0.7 copy-done.4
  40.0 0.7 copy-done.5
  40.7 0.6 shard_map.77
  41.3 0.0 collective-permute-done.1.refs_4_
  41.3 1.5 collective-permute-done.2.refs_5_
  42.8 0.6 collective-permute-done.3.refs_6_
  43.5 0.0 collective-permute-done.4.refs_7_.refs_1_
  43.5 0.5 shard_map.78
  44.0 0.0 copy-start.1
  44.0 9.9 %all_to_all.31 = f32[4,48,256]{2,1,0:T(8,128)S(1)} all-to-all(f32[4,48,256]{2,1,0:T(8,128)S(1)} %get-tuple-element.43), channel_id=1, replica_groups=mesh['y'=4,'z'=32,'core'=2,'grp'=4] {'grp'}, dimensions={0} | all-to-all | bytes 393216 | tf_op jit(solution)/shard_map/all_to_all | solution.py:39
  53.9 0.2 shard_map.80.refs_4_
  54.2 20.8 %collective-permute-start.9 = (f32[48,256]{1,0:T(8,128)S(1)}, f32[48,256]{1,0:T(8,128)S(1)}, u32[]{:S(2)}, u32[]{:S(2)}) collective-permute-start(f32[48,256]{1,0:T(8,128)S(1)} %shard_map.80.refs_4_), channel_id=1, source_target_pairs={{4,68},{12,76},{20,84},{28,92},{36,100},{44,108},{52,116},{60,124}... | collective-permute-start | bytes 147464 | tf_op jit(solution)/shard_map/ppermute | solution.py:27
  74.9 1.3 collective-permute-start.8
  76.2 11.8 %collective-permute-start.7 = (f32[48,256]{1,0:T(8,128)S(1)}, f32[48,256]{1,0:T(8,128)S(1)}, u32[]{:S(2)}, u32[]{:S(2)}) collective-permute-start(f32[48,256]{1,0:T(8,128)S(1)} %shard_map.80.refs_4_), channel_id=1, source_target_pairs={{4,8},{8,4},{12,16},{16,12},{20,24},{24,20},{28,32},{32,28},{36,40... | collective-permute-start | bytes 147464 | tf_op jit(solution)/shard_map/ppermute | solution.py:27
  88.0 1.9 collective-permute-start.6
  90.0 0.9 shard_map.79.refs_3_
  90.9 0.3 shard_map.81
  91.2 1.5 collective-permute-done.8.refs_7_
  92.7 0.0 collective-permute-done.7.refs_6_
  92.7 0.0 collective-permute-done.6.refs_5_
  92.7 1.3 shard_map.82
  94.0 1.3 collective-permute-start.12
  95.3 12.7 %collective-permute-start.13 = (f32[96,256]{1,0:T(8,128)S(1)}, f32[96,256]{1,0:T(8,128)S(1)}, u32[]{:S(2)}, u32[]{:S(2)}) collective-permute-start(f32[96,256]{1,0:T(8,128)S(1)} %get-tuple-element.50.refs_5_), channel_id=1, source_target_pairs={{4,68},{12,76},{20,84},{28,92},{36,100},{44,108},{52,116},{60,124}... | collective-permute-start | bytes 294920 | tf_op jit(solution)/shard_map/ppermute | solution.py:27
  108.0 1.2 shard_map.83
  109.2 1.9 collective-permute-start.10
  111.1 1.9 collective-permute-start.11
  113.0 2.2 collective-permute-start.14
  115.2 0.0 collective-permute-done.12.refs_10_
  115.3 1.3 collective-permute-start.15
  116.6 0.0 collective-permute-done.13.refs_11_
  116.6 0.8 collective-permute-done.11.refs_9_
  117.3 0.2 collective-permute-done.14.refs_12_
  117.5 4.4 %collective-permute-done.15.refs_13_ = f32[96,256]{1,0:T(8,128)S(1)} collective-permute-done((f32[96,256]{1,0:T(8,128)S(1)}, f32[96,256]{1,0:T(8,128)S(1)}, u32[]{:S(2)}, u32[]{:S(2)}) %collective-permute-start.15) | collective-permute-done | bytes 98336 | tf_op jit(solution)/shard_map/ppermute | solution.py:27
  121.9 0.5 shard_map.84
  122.5 8.0 %all_to_all.32 = f32[4,48,256]{2,1,0:T(8,128)S(1)} all-to-all(f32[4,48,256]{2,1,0:T(8,128)S(1)} %get-tuple-element.57), channel_id=1, replica_groups=mesh['y'=4,'z'=32,'core'=2,'grp'=4] {'grp'}, dimensions={0} | all-to-all | bytes 393216 | tf_op jit(solution)/shard_map/all_to_all | solution.py:39
  130.5 0.2 shard_map.86.refs_7_
  130.8 10.6 %collective-permute-start.19 = (f32[48,256]{1,0:T(8,128)S(1)}, f32[48,256]{1,0:T(8,128)S(1)}, u32[]{:S(2)}, u32[]{:S(2)}) collective-permute-start(f32[48,256]{1,0:T(8,128)S(1)} %shard_map.86.refs_7_), channel_id=1, source_target_pairs={{4,68},{12,76},{20,84},{28,92},{36,100},{44,108},{52,116},{60,124}... | collective-permute-start | bytes 147464 | tf_op jit(solution)/shard_map/ppermute | solution.py:27
  141.3 1.3 collective-permute-start.18
  142.6 7.9 %collective-permute-start.17 = (f32[48,256]{1,0:T(8,128)S(1)}, f32[48,256]{1,0:T(8,128)S(1)}, u32[]{:S(2)}, u32[]{:S(2)}) collective-permute-start(f32[48,256]{1,0:T(8,128)S(1)} %shard_map.86.refs_7_), channel_id=1, source_target_pairs={{4,8},{8,4},{12,16},{16,12},{20,24},{24,20},{28,32},{32,28},{36,40... | collective-permute-start | bytes 147464 | tf_op jit(solution)/shard_map/ppermute | solution.py:27
  150.5 1.9 collective-permute-start.16
  152.4 1.6 shard_map.85
  154.1 0.3 shard_map.87
  154.4 0.0 collective-permute-done.19.refs_11_
  154.4 3.8 %collective-permute-done.18.refs_10_ = f32[48,256]{1,0:T(8,128)S(1)} collective-permute-done((f32[48,256]{1,0:T(8,128)S(1)}, f32[48,256]{1,0:T(8,128)S(1)}, u32[]{:S(2)}, u32[]{:S(2)}) %collective-permute-start.18) | collective-permute-done | bytes 49184 | tf_op jit(solution)/shard_map/ppermute | solution.py:27
  158.1 0.0 collective-permute-done.17.refs_9_
  158.1 0.0 collective-permute-done.16.refs_8_
  158.2 2.3 %shard_map.88 = (f32[576,256]{1,0:T(8,128)S(1)}, f32[6,256]{1,0:T(8,128)S(1)}) custom-call(f32[16,256]{1,0:T(8,128)S(1)} %get-tuple-element.33.refs_0_.refs_1_, f32[576,256]{1,0:T(8,128)S(1)} %get-tuple-element.53.refs_1_, f32[576,576]{1,0:T(8,128)S(1)} %bitcast.23, f32[576,96]{1,0:T(8,128)S(1)} %shard_map.79.refs_3_, ...), custom_call_target="tpu_custom_call" | custom-call | flops 1189085184 | bytes 4276224 | tf_op jit(solution)/shard_map/pallas_call | solution.py:66
  160.5 0.1 all_to_all.22
  160.5 19.7 %all_to_all.33 = f32[32,1,48]{2,1,0:T(1,128)S(1)} all-to-all(f32[32,1,48]{2,1,0:T(1,128)S(1)} %bitcast.33), channel_id=1, replica_groups=mesh['y'=4,'z'=32,'core'=2,'grp'=4] {'y','core','grp'}, dimensions={0} | all-to-all | bytes 12288 | tf_op jit(solution)/shard_map/all_to_all | solution.py:39
  180.3 0.1 reduce_sum.18
  180.3 31.0 %all_to_all.34 = f32[32,1,48]{2,1,0:T(1,128)S(1)} all-to-all(f32[32,1,48]{2,1,0:T(1,128)S(1)} %broadcast_in_dim.7), channel_id=1, replica_groups=mesh['y'=4,'z'=32,'core'=2,'grp'=4] {'z'}, dimensions={0} | all-to-all | bytes 12288 | tf_op jit(solution)/shard_map/all_to_all | solution.py:39
  211.4 12.0 %all_to_all.35.refs_1_ = f32[32,1,48]{2,1,0:T(1,128)S(1)} all-to-all(f32[32,1,48]{2,1,0:T(1,128)S(1)} %broadcast_in_dim.8), channel_id=1, replica_groups=mesh['y'=4,'z'=32,'core'=2,'grp'=4] {'y','core','grp'}, dimensions={0} | all-to-all | bytes 12288 | tf_op jit(solution)/shard_map/all_to_all | solution.py:39
  223.4 1.2 shard_map.89
  (12 shorter events, 0.1 us)
Async XLA Ops:
  2.8 21.9 %collective-permute-start = (f32[120,256]{1,0:T(8,128)}, f32[120,256]{1,0:T(8,128)S(1)}, u32[]{:S(2)}, u32[]{:S(2)}) collective-permute-start(f32[120,256]{1,0:T(8,128)} %get-tuple-element.36), channel_id=1, source_target_pairs={{0,4},{4,0},{8,12},{12,8},{16,20},{20,16},{24,28},{28,24},{32,36},... | collective-permute-start | bytes 368648 | tf_op jit(solution)/shard_map/ppermute | solution.py:27
  18.8 24.6 %collective-permute-start.4 = (f32[168,256]{1,0:T(8,128)}, f32[168,256]{1,0:T(8,128)S(1)}, u32[]{:S(2)}, u32[]{:S(2)}) collective-permute-start(f32[168,256]{1,0:T(8,128)} %get-tuple-element.40), channel_id=1, source_target_pairs={{0,1},{1,2},{2,3},{4,5},{5,6},{6,7},{8,9},{9,10},{10,11},{12,13},{... | collective-permute-start | bytes 516104 | tf_op jit(solution)/shard_map/ppermute | solution.py:27
  20.1 23.3 %collective-permute-start.5 = (f32[168,256]{1,0:T(8,128)}, f32[168,256]{1,0:T(8,128)S(1)}, u32[]{:S(2)}, u32[]{:S(2)}) collective-permute-start(f32[168,256]{1,0:T(8,128)} %get-tuple-element.41), channel_id=1, source_target_pairs={{1,0},{2,1},{3,2},{5,4},{6,5},{7,6},{9,8},{10,9},{11,10},{13,12},{... | collective-permute-start | bytes 516104 | tf_op jit(solution)/shard_map/ppermute | solution.py:27
  21.4 19.8 %collective-permute-start.1 = (f32[120,256]{1,0:T(8,128)}, f32[120,256]{1,0:T(8,128)S(1)}, u32[]{:S(2)}, u32[]{:S(2)}) collective-permute-start(f32[120,256]{1,0:T(8,128)} %get-tuple-element.37), channel_id=1, source_target_pairs={{4,8},{8,4},{12,16},{16,12},{20,24},{24,20},{28,32},{32,28},{36,40... | collective-permute-start | bytes 368648 | tf_op jit(solution)/shard_map/ppermute | solution.py:27
  23.4 19.5 %collective-permute-start.2 = (f32[120,256]{1,0:T(8,128)}, f32[120,256]{1,0:T(8,128)S(1)}, u32[]{:S(2)}, u32[]{:S(2)}) collective-permute-start(f32[120,256]{1,0:T(8,128)} %get-tuple-element.38), channel_id=1, source_target_pairs={{0,64},{8,72},{16,80},{24,88},{32,96},{40,104},{48,112},{56,120},{... | collective-permute-start | bytes 368648 | tf_op jit(solution)/shard_map/ppermute | solution.py:27
  24.7 18.8 %collective-permute-start.3 = (f32[120,256]{1,0:T(8,128)}, f32[120,256]{1,0:T(8,128)S(1)}, u32[]{:S(2)}, u32[]{:S(2)}) collective-permute-start(f32[120,256]{1,0:T(8,128)} %get-tuple-element.39), channel_id=1, source_target_pairs={{4,68},{12,76},{20,84},{28,92},{36,100},{44,108},{52,116},{60,124}... | collective-permute-start | bytes 368648 | tf_op jit(solution)/shard_map/ppermute | solution.py:27
  37.4 1.1 copy-start
  38.5 0.9 copy-start.2
  39.4 0.7 copy-start.4
  40.0 0.7 copy-start.5
  40.7 13.3 %copy-start.3 = (f32[1,1,48,192]{3,2,1,0:T(8,128)S(1)}, f32[1,1,48,192]{3,2,1,0:T(8,128)}, u32[]{:S(2)}) copy-start(f32[1,1,48,192]{3,2,1,0:T(8,128)} %param.9) | copy-start | bytes 110596
  44.0 48.7 %copy-start.1 = (f32[1,1,576,576]{3,2,1,0:T(8,128)S(1)}, f32[1,1,576,576]{3,2,1,0:T(8,128)}, u32[]{:S(2)}) copy-start(f32[1,1,576,576]{3,2,1,0:T(8,128)} %param.6) | copy-start | bytes 3981316
  54.2 37.0 %collective-permute-start.9 = (f32[48,256]{1,0:T(8,128)S(1)}, f32[48,256]{1,0:T(8,128)S(1)}, u32[]{:S(2)}, u32[]{:S(2)}) collective-permute-start(f32[48,256]{1,0:T(8,128)S(1)} %shard_map.80.refs_4_), channel_id=1, source_target_pairs={{4,68},{12,76},{20,84},{28,92},{36,100},{44,108},{52,116},{60,124}... | collective-permute-start | bytes 147464 | tf_op jit(solution)/shard_map/ppermute | solution.py:27
  74.9 17.7 %collective-permute-start.8 = (f32[48,256]{1,0:T(8,128)S(1)}, f32[48,256]{1,0:T(8,128)S(1)}, u32[]{:S(2)}, u32[]{:S(2)}) collective-permute-start(f32[48,256]{1,0:T(8,128)S(1)} %shard_map.80.refs_4_), channel_id=1, source_target_pairs={{0,64},{8,72},{16,80},{24,88},{32,96},{40,104},{48,112},{56,120},{... | collective-permute-start | bytes 147464 | tf_op jit(solution)/shard_map/ppermute | solution.py:27
  76.2 16.4 %collective-permute-start.7 = (f32[48,256]{1,0:T(8,128)S(1)}, f32[48,256]{1,0:T(8,128)S(1)}, u32[]{:S(2)}, u32[]{:S(2)}) collective-permute-start(f32[48,256]{1,0:T(8,128)S(1)} %shard_map.80.refs_4_), channel_id=1, source_target_pairs={{4,8},{8,4},{12,16},{16,12},{20,24},{24,20},{28,32},{32,28},{36,40... | collective-permute-start | bytes 147464 | tf_op jit(solution)/shard_map/ppermute | solution.py:27
  88.0 4.6 %collective-permute-start.6 = (f32[48,256]{1,0:T(8,128)S(1)}, f32[48,256]{1,0:T(8,128)S(1)}, u32[]{:S(2)}, u32[]{:S(2)}) collective-permute-start(f32[48,256]{1,0:T(8,128)S(1)} %shard_map.80.refs_4_), channel_id=1, source_target_pairs={{0,4},{4,0},{8,12},{12,8},{16,20},{20,16},{24,28},{28,24},{32,36},... | collective-permute-start | bytes 147464 | tf_op jit(solution)/shard_map/ppermute | solution.py:27
  94.0 21.3 %collective-permute-start.12 = (f32[96,256]{1,0:T(8,128)S(1)}, f32[96,256]{1,0:T(8,128)S(1)}, u32[]{:S(2)}, u32[]{:S(2)}) collective-permute-start(f32[96,256]{1,0:T(8,128)S(1)} %get-tuple-element.49.refs_4_), channel_id=1, source_target_pairs={{0,64},{8,72},{16,80},{24,88},{32,96},{40,104},{48,112},{56,120},{... | collective-permute-start | bytes 294920 | tf_op jit(solution)/shard_map/ppermute | solution.py:27
  95.3 21.3 %collective-permute-start.13 = (f32[96,256]{1,0:T(8,128)S(1)}, f32[96,256]{1,0:T(8,128)S(1)}, u32[]{:S(2)}, u32[]{:S(2)}) collective-permute-start(f32[96,256]{1,0:T(8,128)S(1)} %get-tuple-element.50.refs_5_), channel_id=1, source_target_pairs={{4,68},{12,76},{20,84},{28,92},{36,100},{44,108},{52,116},{60,124}... | collective-permute-start | bytes 294920 | tf_op jit(solution)/shard_map/ppermute | solution.py:27
  109.2 7.4 %collective-permute-start.10 = (f32[96,256]{1,0:T(8,128)S(1)}, f32[96,256]{1,0:T(8,128)S(1)}, u32[]{:S(2)}, u32[]{:S(2)}) collective-permute-start(f32[96,256]{1,0:T(8,128)S(1)} %get-tuple-element.47.refs_2_), channel_id=1, source_target_pairs={{0,4},{4,0},{8,12},{12,8},{16,20},{20,16},{24,28},{28,24},{32,36},... | collective-permute-start | bytes 294920 | tf_op jit(solution)/shard_map/ppermute | solution.py:27
  111.1 6.2 %collective-permute-start.11 = (f32[96,256]{1,0:T(8,128)S(1)}, f32[96,256]{1,0:T(8,128)S(1)}, u32[]{:S(2)}, u32[]{:S(2)}) collective-permute-start(f32[96,256]{1,0:T(8,128)S(1)} %get-tuple-element.48.refs_3_), channel_id=1, source_target_pairs={{4,8},{8,4},{12,16},{16,12},{20,24},{24,20},{28,32},{32,28},{36,40... | collective-permute-start | bytes 294920 | tf_op jit(solution)/shard_map/ppermute | solution.py:27
  113.0 4.5 %collective-permute-start.14 = (f32[96,256]{1,0:T(8,128)S(1)}, f32[96,256]{1,0:T(8,128)S(1)}, u32[]{:S(2)}, u32[]{:S(2)}) collective-permute-start(f32[96,256]{1,0:T(8,128)S(1)} %get-tuple-element.51.refs_6_), channel_id=1, source_target_pairs={{0,1},{1,2},{2,3},{4,5},{5,6},{6,7},{8,9},{9,10},{10,11},{12,13},{... | collective-permute-start | bytes 294920 | tf_op jit(solution)/shard_map/ppermute | solution.py:27
  115.3 6.7 %collective-permute-start.15 = (f32[96,256]{1,0:T(8,128)S(1)}, f32[96,256]{1,0:T(8,128)S(1)}, u32[]{:S(2)}, u32[]{:S(2)}) collective-permute-start(f32[96,256]{1,0:T(8,128)S(1)} %get-tuple-element.52.refs_7_), channel_id=1, source_target_pairs={{1,0},{2,1},{3,2},{5,4},{6,5},{7,6},{9,8},{10,9},{11,10},{13,12},{... | collective-permute-start | bytes 294920 | tf_op jit(solution)/shard_map/ppermute | solution.py:27
  130.8 23.6 %collective-permute-start.19 = (f32[48,256]{1,0:T(8,128)S(1)}, f32[48,256]{1,0:T(8,128)S(1)}, u32[]{:S(2)}, u32[]{:S(2)}) collective-permute-start(f32[48,256]{1,0:T(8,128)S(1)} %shard_map.86.refs_7_), channel_id=1, source_target_pairs={{4,68},{12,76},{20,84},{28,92},{36,100},{44,108},{52,116},{60,124}... | collective-permute-start | bytes 147464 | tf_op jit(solution)/shard_map/ppermute | solution.py:27
  141.3 16.8 %collective-permute-start.18 = (f32[48,256]{1,0:T(8,128)S(1)}, f32[48,256]{1,0:T(8,128)S(1)}, u32[]{:S(2)}, u32[]{:S(2)}) collective-permute-start(f32[48,256]{1,0:T(8,128)S(1)} %shard_map.86.refs_7_), channel_id=1, source_target_pairs={{0,64},{8,72},{16,80},{24,88},{32,96},{40,104},{48,112},{56,120},{... | collective-permute-start | bytes 147464 | tf_op jit(solution)/shard_map/ppermute | solution.py:27
  142.6 15.5 %collective-permute-start.17 = (f32[48,256]{1,0:T(8,128)S(1)}, f32[48,256]{1,0:T(8,128)S(1)}, u32[]{:S(2)}, u32[]{:S(2)}) collective-permute-start(f32[48,256]{1,0:T(8,128)S(1)} %shard_map.86.refs_7_), channel_id=1, source_target_pairs={{4,8},{8,4},{12,16},{16,12},{20,24},{24,20},{28,32},{32,28},{36,40... | collective-permute-start | bytes 147464 | tf_op jit(solution)/shard_map/ppermute | solution.py:27
  150.5 7.7 %collective-permute-start.16 = (f32[48,256]{1,0:T(8,128)S(1)}, f32[48,256]{1,0:T(8,128)S(1)}, u32[]{:S(2)}, u32[]{:S(2)}) collective-permute-start(f32[48,256]{1,0:T(8,128)S(1)} %shard_map.86.refs_7_), channel_id=1, source_target_pairs={{0,4},{4,0},{8,12},{12,8},{16,20},{20,16},{24,28},{28,24},{32,36},... | collective-permute-start | bytes 147464 | tf_op jit(solution)/shard_map/ppermute | solution.py:27
where the time goes:
time: 226 us; the launch traced here: 225 us
  starting transfers between devices  113 us (50%)
  blocking collectives  80.8 us (36%)
  Pallas kernels  13.4 us (6%)
  waiting for transfers between devices  12.8 us (6%)
  local copies, waits for them, and re-layouts  3.38 us (1%)
    ppermute x20, starting transfers between devices, fetch(): return lax.ppermute(piece, axis, pairs)  113 us
    all_to_all x5, blocking collectives, swap(): return lax.all_to_all(blocks, axes, 0, 0, tiled=True)  80.8 us
    ppermute x20, waiting for transfers between devices, fetch(): return lax.ppermute(piece, axis, pairs)  12.8 us
    pallas_call x13, Pallas kernels, kernel_call(): pl.pallas_call(functools.partial(body, len(flags), len(arrays)), out_shap...  11.3 us
  transfers between devices with their start and end apart: 20, of which 7 were waited for; matrix products, arithmetic and copies ran while one was open for 0% of the time, Pallas kernels for 2%

commit v1 on v0

--- a/solution.py
+++ b/solution.py
@@ -15,15 +15,21 @@
 CORE = 6
 PLANE = ("y", "core", "grp")
 SUB = ("y", "z", "core")
-SOURCES = ((SUB, -1), (SUB, 1), (SUB, -SUBROW), (SUB, SUBROW), ("grp", -1), ("grp", 1))
+GRP = ("core", "grp")
+SOURCES = ((SUB, -1), (SUB, 1), (SUB, -SUBROW), (SUB, SUBROW), (GRP, -1), (GRP, 1))
 ORDER = (2, 3, 1, 4, 5, 0)
 
 
 def fetch(piece, slot):
     axis, offset = SOURCES[slot]
     count = lax.axis_size(axis)
-    turned = [1 - 2 * (i % 2) if axis == SUB else 1 for i in range(count)]
-    pairs = [(i, i - offset * turned[i]) for i in range(count) if 0 <= i - offset * turned[i] < count]
+    span = lax.axis_size("grp") if axis == GRP else count
+    pairs = []
+    for i in range(count):
+        core = i // span if axis == GRP else i % 2
+        at = i % span - offset * (1 - 2 * core)
+        if 0 <= at < span:
+            pairs.append((i, i - i % span + at))
     return lax.ppermute(piece, axis, pairs)
 
 
@@ -79,13 +85,13 @@
 
 def unturned(second, arrays, received):
     turned = []
-    for lower, upper in ((0, 1), (2, 3)):
+    for lower, upper in ((0, 1), (2, 3), (4, 5)):
         low, up = arrays[lower], arrays[upper]
         if received and lower == 0:
             low, up = up, low
         turned.append(jnp.where(second, up, low))
         turned.append(jnp.where(second, low, up))
-    return turned + list(arrays[4:])
+    return turned
 
 
 def pack_kernel(gap, shapes, rows, *refs):
@@ -98,7 +104,7 @@
         pltpu.make_async_copy(rows, rows_here, sems.at[1]),
     ]
     for slot, out in enumerate(outs):
-        turn = 0 if slot >= 4 else core if slot % 2 else -core
+        turn = core if slot % 2 else -core
         at = ((slot ^ 1) + turn) * face
         piece = gap.at[pl.ds(pl.multiple_of(at, 8), face)]
         copies.append(pltpu.make_async_copy(piece, out.at[pl.ds(0, face)], sems.at[2 + slot]))
@@ -234,8 +240,8 @@
     lower = dot(operator[4 * face:], push[...])
     outs[0][...] = jnp.where(second, upper[:face], upper[face:])
     outs[1][...] = jnp.where(second, upper[face:], upper[:face])
-    outs[2][...] = lower[face:]
-    outs[3][...] = lower[:face]
+    outs[2][...] = jnp.where(second, lower[:face], lower[face:])
+    outs[3][...] = jnp.where(second, lower[face:], lower[:face])
 
 
 def inner(left, right):

time: 226 us -> 227 us (level)
  waiting for transfers between devices: 12.8 us -> 4.99 us
  starting transfers between devices: 113 us -> 120 us
    ppermute x20, waiting for transfers between devices: 12.8 us -> 4.99 us  [fetch(): return lax.ppermute(piece, axis, pairs)]
    ppermute x20, starting transfers between devices: 113 us -> 120 us  [fetch(): return lax.ppermute(piece, axis, pairs)]
  transfers between devices with their start and end apart: 20 -> 20, of which waited for: 7 -> 4; matrix products, arithmetic and copies ran while one was open for 0% -> 0% of each run, Pallas kernels for 2% -> 2%
where the time goes in v1:
time: 227 us; the launch traced here: 226 us
  starting transfers between devices  120 us (53%)
  blocking collectives  82.3 us (36%)
  Pallas kernels  13.5 us (6%)
  waiting for transfers between devices  4.99 us (2%)
  local copies, waits for them, and re-layouts  3.38 us (1%)
    ppermute x20, starting transfers between devices, fetch(): return lax.ppermute(piece, axis, pairs)  120 us
    all_to_all x5, blocking collectives, swap(): return lax.all_to_all(blocks, axes, 0, 0, tiled=True)  82.3 us
    pallas_call x13, Pallas kernels, kernel_call(): pl.pallas_call(functools.partial(body, len(flags), len(arrays)), out_shap...  11.3 us
    ppermute x20, waiting for transfers between devices, fetch(): return lax.ppermute(piece, axis, pairs)  4.99 us
  transfers between devices with their start and end apart: 20, of which 4 were waited for; matrix products, arithmetic and copies ran while one was open for 0% of the time, Pallas kernels for 2%

profile of v1, /device:TPU:1, one launch (start us, length us, event | category | flops | bytes accessed | tf_op | source)
XLA Modules:
  0.0 225.6 jit_solution(6460207392368652721)
XLA Ops:
  0.6 2.2 pack.1
  2.8 16.0 %collective-permute-start = (f32[120,256]{1,0:T(8,128)}, f32[120,256]{1,0:T(8,128)S(1)}, u32[]{:S(2)}, u32[]{:S(2)}) collective-permute-start(f32[120,256]{1,0:T(8,128)} %get-tuple-element.36), channel_id=1, source_target_pairs={{0,4},{4,0},{8,12},{12,8},{16,20},{20,16},{24,28},{28,24},{32,36},... | collective-permute-start | bytes 368648 | tf_op jit(solution)/shard_map/ppermute | solution.py:33
  18.8 1.3 collective-permute-start.4
  20.1 4.0 %collective-permute-start.5 = (f32[168,256]{1,0:T(8,128)}, f32[168,256]{1,0:T(8,128)S(1)}, u32[]{:S(2)}, u32[]{:S(2)}) collective-permute-start(f32[168,256]{1,0:T(8,128)} %get-tuple-element.41), channel_id=1, source_target_pairs={{1,0},{2,1},{3,2},{4,5},{5,6},{6,7},{9,8},{10,9},{11,10},{12,13},{... | collective-permute-start | bytes 516104 | tf_op jit(solution)/shard_map/ppermute | solution.py:33
  24.1 1.9 collective-permute-start.1
  26.1 1.3 collective-permute-start.2
  27.4 0.0 collective-permute-done.refs_3_
  27.4 12.7 %collective-permute-start.3 = (f32[120,256]{1,0:T(8,128)}, f32[120,256]{1,0:T(8,128)S(1)}, u32[]{:S(2)}, u32[]{:S(2)}) collective-permute-start(f32[120,256]{1,0:T(8,128)} %get-tuple-element.39), channel_id=1, source_target_pairs={{4,68},{12,76},{20,84},{28,92},{36,100},{44,108},{52,116},{60,124}... | collective-permute-start | bytes 368648 | tf_op jit(solution)/shard_map/ppermute | solution.py:33
  40.1 0.0 copy-start
  40.1 1.1 copy-done
  41.2 0.9 copy-done.2
  42.1 0.7 copy-done.4
  42.7 0.7 copy-done.5
  43.4 0.6 shard_map.77
  44.0 0.0 collective-permute-done.1.refs_4_
  44.0 0.0 collective-permute-done.2.refs_5_
  44.0 0.3 collective-permute-done.3.refs_6_
  44.3 0.0 collective-permute-done.4.refs_7_.refs_1_
  44.3 0.0 collective-permute-done.5.refs_8_.refs_2_
  44.3 0.6 shard_map.78
  44.9 0.0 copy-start.1
  44.9 9.1 %all_to_all.31 = f32[4,48,256]{2,1,0:T(8,128)S(1)} all-to-all(f32[4,48,256]{2,1,0:T(8,128)S(1)} %get-tuple-element.43), channel_id=1, replica_groups=mesh['y'=4,'z'=32,'core'=2,'grp'=4] {'grp'}, dimensions={0} | all-to-all | bytes 393216 | tf_op jit(solution)/shard_map/all_to_all | solution.py:45
  54.0 0.2 shard_map.80.refs_4_
  54.2 20.8 %collective-permute-start.9 = (f32[48,256]{1,0:T(8,128)S(1)}, f32[48,256]{1,0:T(8,128)S(1)}, u32[]{:S(2)}, u32[]{:S(2)}) collective-permute-start(f32[48,256]{1,0:T(8,128)S(1)} %shard_map.80.refs_4_), channel_id=1, source_target_pairs={{4,68},{12,76},{20,84},{28,92},{36,100},{44,108},{52,116},{60,124}... | collective-permute-start | bytes 147464 | tf_op jit(solution)/shard_map/ppermute | solution.py:33
  75.0 1.3 collective-permute-start.8
  76.3 11.8 %collective-permute-start.7 = (f32[48,256]{1,0:T(8,128)S(1)}, f32[48,256]{1,0:T(8,128)S(1)}, u32[]{:S(2)}, u32[]{:S(2)}) collective-permute-start(f32[48,256]{1,0:T(8,128)S(1)} %shard_map.80.refs_4_), channel_id=1, source_target_pairs={{4,8},{8,4},{12,16},{16,12},{20,24},{24,20},{28,32},{32,28},{36,40... | collective-permute-start | bytes 147464 | tf_op jit(solution)/shard_map/ppermute | solution.py:33
  88.1 1.9 collective-permute-start.6
  90.0 0.9 shard_map.79.refs_3_
  90.9 0.3 shard_map.81
  91.2 0.0 collective-permute-done.9.refs_8_
  91.2 1.3 collective-permute-done.8.refs_7_
  92.6 0.0 collective-permute-done.7.refs_6_
  92.6 0.0 collective-permute-done.6.refs_5_
  92.6 1.3 shard_map.82
  93.9 1.3 collective-permute-start.12
  95.2 12.8 %collective-permute-start.13 = (f32[96,256]{1,0:T(8,128)S(1)}, f32[96,256]{1,0:T(8,128)S(1)}, u32[]{:S(2)}, u32[]{:S(2)}) collective-permute-start(f32[96,256]{1,0:T(8,128)S(1)} %get-tuple-element.50.refs_5_), channel_id=1, source_target_pairs={{4,68},{12,76},{20,84},{28,92},{36,100},{44,108},{52,116},{60,124}... | collective-permute-start | bytes 294920 | tf_op jit(solution)/shard_map/ppermute | solution.py:33
  108.0 1.2 shard_map.83
  109.2 1.9 collective-permute-start.10
  111.1 1.9 collective-permute-start.11
  113.0 1.3 collective-permute-start.14
  114.3 0.0 collective-permute-done.12.refs_10_
  114.4 4.0 %collective-permute-start.15 = (f32[96,256]{1,0:T(8,128)S(1)}, f32[96,256]{1,0:T(8,128)S(1)}, u32[]{:S(2)}, u32[]{:S(2)}) collective-permute-start(f32[96,256]{1,0:T(8,128)S(1)} %get-tuple-element.52.refs_7_), channel_id=1, source_target_pairs={{1,0},{2,1},{3,2},{4,5},{5,6},{6,7},{9,8},{10,9},{11,10},{12,13},{... | collective-permute-start | bytes 294920 | tf_op jit(solution)/shard_map/ppermute | solution.py:33
  118.4 0.0 collective-permute-done.13.refs_11_
  118.4 0.0 collective-permute-done.10.refs_8_
  118.4 0.0 collective-permute-done.14.refs_12_
  118.4 1.6 collective-permute-done.15.refs_13_
  120.0 0.6 shard_map.84
  120.6 9.0 %all_to_all.32 = f32[4,48,256]{2,1,0:T(8,128)S(1)} all-to-all(f32[4,48,256]{2,1,0:T(8,128)S(1)} %get-tuple-element.57), channel_id=1, replica_groups=mesh['y'=4,'z'=32,'core'=2,'grp'=4] {'grp'}, dimensions={0} | all-to-all | bytes 393216 | tf_op jit(solution)/shard_map/all_to_all | solution.py:45
  129.5 0.2 shard_map.86.refs_7_
  129.8 12.1 %collective-permute-start.19 = (f32[48,256]{1,0:T(8,128)S(1)}, f32[48,256]{1,0:T(8,128)S(1)}, u32[]{:S(2)}, u32[]{:S(2)}) collective-permute-start(f32[48,256]{1,0:T(8,128)S(1)} %shard_map.86.refs_7_), channel_id=1, source_target_pairs={{4,68},{12,76},{20,84},{28,92},{36,100},{44,108},{52,116},{60,124}... | collective-permute-start | bytes 147464 | tf_op jit(solution)/shard_map/ppermute | solution.py:33
  141.8 1.3 collective-permute-start.18
  143.1 8.8 %collective-permute-start.17 = (f32[48,256]{1,0:T(8,128)S(1)}, f32[48,256]{1,0:T(8,128)S(1)}, u32[]{:S(2)}, u32[]{:S(2)}) collective-permute-start(f32[48,256]{1,0:T(8,128)S(1)} %shard_map.86.refs_7_), channel_id=1, source_target_pairs={{4,8},{8,4},{12,16},{16,12},{20,24},{24,20},{28,32},{32,28},{36,40... | collective-permute-start | bytes 147464 | tf_op jit(solution)/shard_map/ppermute | solution.py:33
  152.0 1.9 collective-permute-start.16
  153.9 1.6 shard_map.85
  155.5 0.3 shard_map.87
  155.8 0.0 collective-permute-done.19.refs_11_
  155.8 1.7 collective-permute-done.18.refs_10_
  157.6 2.3 %shard_map.88 = (f32[576,256]{1,0:T(8,128)S(1)}, f32[6,256]{1,0:T(8,128)S(1)}) custom-call(f32[16,256]{1,0:T(8,128)S(1)} %get-tuple-element.33.refs_0_.refs_1_, f32[576,256]{1,0:T(8,128)S(1)} %get-tuple-element.53.refs_1_, f32[576,576]{1,0:T(8,128)S(1)} %bitcast.23, f32[576,96]{1,0:T(8,128)S(1)} %shard_map.79.refs_3_, ...), custom_call_target="tpu_custom_call" | custom-call | flops 1189085184 | bytes 4276224 | tf_op jit(solution)/shard_map/pallas_call | solution.py:72
  159.9 0.1 all_to_all.22
  159.9 21.7 %all_to_all.33 = f32[32,1,48]{2,1,0:T(1,128)S(1)} all-to-all(f32[32,1,48]{2,1,0:T(1,128)S(1)} %bitcast.33), channel_id=1, replica_groups=mesh['y'=4,'z'=32,'core'=2,'grp'=4] {'y','core','grp'}, dimensions={0} | all-to-all | bytes 12288 | tf_op jit(solution)/shard_map/all_to_all | solution.py:45
  181.7 0.1 reduce_sum.18
  181.8 30.5 %all_to_all.34 = f32[32,1,48]{2,1,0:T(1,128)S(1)} all-to-all(f32[32,1,48]{2,1,0:T(1,128)S(1)} %broadcast_in_dim.7), channel_id=1, replica_groups=mesh['y'=4,'z'=32,'core'=2,'grp'=4] {'z'}, dimensions={0} | all-to-all | bytes 12288 | tf_op jit(solution)/shard_map/all_to_all | solution.py:45
  212.3 12.0 %all_to_all.35.refs_1_ = f32[32,1,48]{2,1,0:T(1,128)S(1)} all-to-all(f32[32,1,48]{2,1,0:T(1,128)S(1)} %broadcast_in_dim.8), channel_id=1, replica_groups=mesh['y'=4,'z'=32,'core'=2,'grp'=4] {'y','core','grp'}, dimensions={0} | all-to-all | bytes 12288 | tf_op jit(solution)/shard_map/all_to_all | solution.py:45
  224.3 1.2 shard_map.89
  (12 shorter events, 0.1 us)
Async XLA Ops:
  2.8 24.6 %collective-permute-start = (f32[120,256]{1,0:T(8,128)}, f32[120,256]{1,0:T(8,128)S(1)}, u32[]{:S(2)}, u32[]{:S(2)}) collective-permute-start(f32[120,256]{1,0:T(8,128)} %get-tuple-element.36), channel_id=1, source_target_pairs={{0,4},{4,0},{8,12},{12,8},{16,20},{20,16},{24,28},{28,24},{32,36},... | collective-permute-start | bytes 368648 | tf_op jit(solution)/shard_map/ppermute | solution.py:33
  18.8 25.5 %collective-permute-start.4 = (f32[168,256]{1,0:T(8,128)}, f32[168,256]{1,0:T(8,128)S(1)}, u32[]{:S(2)}, u32[]{:S(2)}) collective-permute-start(f32[168,256]{1,0:T(8,128)} %get-tuple-element.40), channel_id=1, source_target_pairs={{0,1},{1,2},{2,3},{5,4},{6,5},{7,6},{8,9},{9,10},{10,11},{13,12},{... | collective-permute-start | bytes 516104 | tf_op jit(solution)/shard_map/ppermute | solution.py:33
  20.1 24.2 %collective-permute-start.5 = (f32[168,256]{1,0:T(8,128)}, f32[168,256]{1,0:T(8,128)S(1)}, u32[]{:S(2)}, u32[]{:S(2)}) collective-permute-start(f32[168,256]{1,0:T(8,128)} %get-tuple-element.41), channel_id=1, source_target_pairs={{1,0},{2,1},{3,2},{4,5},{5,6},{6,7},{9,8},{10,9},{11,10},{12,13},{... | collective-permute-start | bytes 516104 | tf_op jit(solution)/shard_map/ppermute | solution.py:33
  24.1 19.8 %collective-permute-start.1 = (f32[120,256]{1,0:T(8,128)}, f32[120,256]{1,0:T(8,128)S(1)}, u32[]{:S(2)}, u32[]{:S(2)}) collective-permute-start(f32[120,256]{1,0:T(8,128)} %get-tuple-element.37), channel_id=1, source_target_pairs={{4,8},{8,4},{12,16},{16,12},{20,24},{24,20},{28,32},{32,28},{36,40... | collective-permute-start | bytes 368648 | tf_op jit(solution)/shard_map/ppermute | solution.py:33
  26.1 17.9 %collective-permute-start.2 = (f32[120,256]{1,0:T(8,128)}, f32[120,256]{1,0:T(8,128)S(1)}, u32[]{:S(2)}, u32[]{:S(2)}) collective-permute-start(f32[120,256]{1,0:T(8,128)} %get-tuple-element.38), channel_id=1, source_target_pairs={{0,64},{8,72},{16,80},{24,88},{32,96},{40,104},{48,112},{56,120},{... | collective-permute-start | bytes 368648 | tf_op jit(solution)/shard_map/ppermute | solution.py:33
  27.4 16.9 %collective-permute-start.3 = (f32[120,256]{1,0:T(8,128)}, f32[120,256]{1,0:T(8,128)S(1)}, u32[]{:S(2)}, u32[]{:S(2)}) collective-permute-start(f32[120,256]{1,0:T(8,128)} %get-tuple-element.39), channel_id=1, source_target_pairs={{4,68},{12,76},{20,84},{28,92},{36,100},{44,108},{52,116},{60,124}... | collective-permute-start | bytes 368648 | tf_op jit(solution)/shard_map/ppermute | solution.py:33
  40.1 1.1 copy-start
  41.2 0.9 copy-start.2
  42.1 0.7 copy-start.4
  42.7 0.7 copy-start.5
  43.4 10.6 %copy-start.3 = (f32[1,1,48,192]{3,2,1,0:T(8,128)S(1)}, f32[1,1,48,192]{3,2,1,0:T(8,128)}, u32[]{:S(2)}) copy-start(f32[1,1,48,192]{3,2,1,0:T(8,128)} %param.9) | copy-start | bytes 110596
  44.9 47.7 %copy-start.1 = (f32[1,1,576,576]{3,2,1,0:T(8,128)S(1)}, f32[1,1,576,576]{3,2,1,0:T(8,128)}, u32[]{:S(2)}) copy-start(f32[1,1,576,576]{3,2,1,0:T(8,128)} %param.6) | copy-start | bytes 3981316
  54.2 37.1 %collective-permute-start.9 = (f32[48,256]{1,0:T(8,128)S(1)}, f32[48,256]{1,0:T(8,128)S(1)}, u32[]{:S(2)}, u32[]{:S(2)}) collective-permute-start(f32[48,256]{1,0:T(8,128)S(1)} %shard_map.80.refs_4_), channel_id=1, source_target_pairs={{4,68},{12,76},{20,84},{28,92},{36,100},{44,108},{52,116},{60,124}... | collective-permute-start | bytes 147464 | tf_op jit(solution)/shard_map/ppermute | solution.py:33
  75.0 17.6 %collective-permute-start.8 = (f32[48,256]{1,0:T(8,128)S(1)}, f32[48,256]{1,0:T(8,128)S(1)}, u32[]{:S(2)}, u32[]{:S(2)}) collective-permute-start(f32[48,256]{1,0:T(8,128)S(1)} %shard_map.80.refs_4_), channel_id=1, source_target_pairs={{0,64},{8,72},{16,80},{24,88},{32,96},{40,104},{48,112},{56,120},{... | collective-permute-start | bytes 147464 | tf_op jit(solution)/shard_map/ppermute | solution.py:33
  76.3 16.3 %collective-permute-start.7 = (f32[48,256]{1,0:T(8,128)S(1)}, f32[48,256]{1,0:T(8,128)S(1)}, u32[]{:S(2)}, u32[]{:S(2)}) collective-permute-start(f32[48,256]{1,0:T(8,128)S(1)} %shard_map.80.refs_4_), channel_id=1, source_target_pairs={{4,8},{8,4},{12,16},{16,12},{20,24},{24,20},{28,32},{32,28},{36,40... | collective-permute-start | bytes 147464 | tf_op jit(solution)/shard_map/ppermute | solution.py:33
  88.1 4.5 %collective-permute-start.6 = (f32[48,256]{1,0:T(8,128)S(1)}, f32[48,256]{1,0:T(8,128)S(1)}, u32[]{:S(2)}, u32[]{:S(2)}) collective-permute-start(f32[48,256]{1,0:T(8,128)S(1)} %shard_map.80.refs_4_), channel_id=1, source_target_pairs={{0,4},{4,0},{8,12},{12,8},{16,20},{20,16},{24,28},{28,24},{32,36},... | collective-permute-start | bytes 147464 | tf_op jit(solution)/shard_map/ppermute | solution.py:33
  93.9 20.5 %collective-permute-start.12 = (f32[96,256]{1,0:T(8,128)S(1)}, f32[96,256]{1,0:T(8,128)S(1)}, u32[]{:S(2)}, u32[]{:S(2)}) collective-permute-start(f32[96,256]{1,0:T(8,128)S(1)} %get-tuple-element.49.refs_4_), channel_id=1, source_target_pairs={{0,64},{8,72},{16,80},{24,88},{32,96},{40,104},{48,112},{56,120},{... | collective-permute-start | bytes 294920 | tf_op jit(solution)/shard_map/ppermute | solution.py:33
  95.2 23.2 %collective-permute-start.13 = (f32[96,256]{1,0:T(8,128)S(1)}, f32[96,256]{1,0:T(8,128)S(1)}, u32[]{:S(2)}, u32[]{:S(2)}) collective-permute-start(f32[96,256]{1,0:T(8,128)S(1)} %get-tuple-element.50.refs_5_), channel_id=1, source_target_pairs={{4,68},{12,76},{20,84},{28,92},{36,100},{44,108},{52,116},{60,124}... | collective-permute-start | bytes 294920 | tf_op jit(solution)/shard_map/ppermute | solution.py:33
  109.2 9.2 %collective-permute-start.10 = (f32[96,256]{1,0:T(8,128)S(1)}, f32[96,256]{1,0:T(8,128)S(1)}, u32[]{:S(2)}, u32[]{:S(2)}) collective-permute-start(f32[96,256]{1,0:T(8,128)S(1)} %get-tuple-element.47.refs_2_), channel_id=1, source_target_pairs={{0,4},{4,0},{8,12},{12,8},{16,20},{20,16},{24,28},{28,24},{32,36},... | collective-permute-start | bytes 294920 | tf_op jit(solution)/shard_map/ppermute | solution.py:33
  111.1 7.3 %collective-permute-start.11 = (f32[96,256]{1,0:T(8,128)S(1)}, f32[96,256]{1,0:T(8,128)S(1)}, u32[]{:S(2)}, u32[]{:S(2)}) collective-permute-start(f32[96,256]{1,0:T(8,128)S(1)} %get-tuple-element.48.refs_3_), channel_id=1, source_target_pairs={{4,8},{8,4},{12,16},{16,12},{20,24},{24,20},{28,32},{32,28},{36,40... | collective-permute-start | bytes 294920 | tf_op jit(solution)/shard_map/ppermute | solution.py:33
  113.0 5.4 %collective-permute-start.14 = (f32[96,256]{1,0:T(8,128)S(1)}, f32[96,256]{1,0:T(8,128)S(1)}, u32[]{:S(2)}, u32[]{:S(2)}) collective-permute-start(f32[96,256]{1,0:T(8,128)S(1)} %get-tuple-element.51.refs_6_), channel_id=1, source_target_pairs={{0,1},{1,2},{2,3},{5,4},{6,5},{7,6},{8,9},{9,10},{10,11},{13,12},{... | collective-permute-start | bytes 294920 | tf_op jit(solution)/shard_map/ppermute | solution.py:33
  114.4 5.6 %collective-permute-start.15 = (f32[96,256]{1,0:T(8,128)S(1)}, f32[96,256]{1,0:T(8,128)S(1)}, u32[]{:S(2)}, u32[]{:S(2)}) collective-permute-start(f32[96,256]{1,0:T(8,128)S(1)} %get-tuple-element.52.refs_7_), channel_id=1, source_target_pairs={{1,0},{2,1},{3,2},{4,5},{5,6},{6,7},{9,8},{10,9},{11,10},{12,13},{... | collective-permute-start | bytes 294920 | tf_op jit(solution)/shard_map/ppermute | solution.py:33
  129.8 26.1 %collective-permute-start.19 = (f32[48,256]{1,0:T(8,128)S(1)}, f32[48,256]{1,0:T(8,128)S(1)}, u32[]{:S(2)}, u32[]{:S(2)}) collective-permute-start(f32[48,256]{1,0:T(8,128)S(1)} %shard_map.86.refs_7_), channel_id=1, source_target_pairs={{4,68},{12,76},{20,84},{28,92},{36,100},{44,108},{52,116},{60,124}... | collective-permute-start | bytes 147464 | tf_op jit(solution)/shard_map/ppermute | solution.py:33
  141.8 15.7 %collective-permute-start.18 = (f32[48,256]{1,0:T(8,128)S(1)}, f32[48,256]{1,0:T(8,128)S(1)}, u32[]{:S(2)}, u32[]{:S(2)}) collective-permute-start(f32[48,256]{1,0:T(8,128)S(1)} %shard_map.86.refs_7_), channel_id=1, source_target_pairs={{0,64},{8,72},{16,80},{24,88},{32,96},{40,104},{48,112},{56,120},{... | collective-permute-start | bytes 147464 | tf_op jit(solution)/shard_map/ppermute | solution.py:33
  143.1 14.4 %collective-permute-start.17 = (f32[48,256]{1,0:T(8,128)S(1)}, f32[48,256]{1,0:T(8,128)S(1)}, u32[]{:S(2)}, u32[]{:S(2)}) collective-permute-start(f32[48,256]{1,0:T(8,128)S(1)} %shard_map.86.refs_7_), channel_id=1, source_target_pairs={{4,8},{8,4},{12,16},{16,12},{20,24},{24,20},{28,32},{32,28},{36,40... | collective-permute-start | bytes 147464 | tf_op jit(solution)/shard_map/ppermute | solution.py:33
  152.0 5.6 %collective-permute-start.16 = (f32[48,256]{1,0:T(8,128)S(1)}, f32[48,256]{1,0:T(8,128)S(1)}, u32[]{:S(2)}, u32[]{:S(2)}) collective-permute-start(f32[48,256]{1,0:T(8,128)S(1)} %shard_map.86.refs_7_), channel_id=1, source_target_pairs={{0,4},{4,0},{8,12},{12,8},{16,20},{20,16},{24,28},{28,24},{32,36},... | collective-permute-start | bytes 147464 | tf_op jit(solution)/shard_map/ppermute | solution.py:33
